TPU v7x, 256 devices: a whole 4x4x8 slice. The times are simulated.
256 devices in a mesh: grp: 4 (over y), seq: 64 (over z, x, core).
Axes of the slice: x: 4, y: 4, z: 8, core: 2. Of those that a mesh axis runs over, the one named last changes fastest.
Arguments:
- tokens: bfloat16 [1024, 1024], P(('grp', 'seq')), may hold values from -6 to 6
- attn_gain: float32 [1024], replicated, may hold values from 0.1 to 1.9
- w_qkv: bfloat16 [1024, 3072], replicated, may hold values from -0.1875 to 0.1875
- w_out: bfloat16 [1024, 1024], replicated, may hold values from -0.1875 to 0.1875
- mlp_gain: float32 [1024], replicated, may hold values from 0.1 to 1.9
- w_gate_up: bfloat16 [2, 1024, 4096], P(None, None, 'seq'), may hold values from -0.1875 to 0.1875
- w_down: bfloat16 [4096, 1024], P('seq'), may hold values from -0.09375 to 0.09375
- kv_cache: bfloat16 [3072, 2, 64, 1024], P(('grp', 'seq'))
- block_owner: int32 [3072], P(('grp', 'seq')), may hold values from 0 to 255, as said below
- block_fill: int32 [3072], P(('grp', 'seq')), may hold values from 0 to 64, as said below
Outputs:
- output: bfloat16 [1024, 1024], P(('grp', 'seq'))
Inputs may be any that keep to these rules, and one draw needn't show every extreme that they name: `block_fill`: each request has at least one block; in each group one request fills exactly 256 whole blocks, every other has at most 2 blocks; blocks of one request are live from their start and all but its last are full; blocks with no live token exist in every group. `block_owner`: every served request number of a group names some block of that group.
All inputs are finite; a program needn't handle non-finite values.
Results may differ from a plain program's by a relative error of at most 0.024.
Values may be sent and summed in bfloat16 or wider, within the bound.
No kernel may reach another device: no remote copies, remote signals or barrier semaphores. Data moves between devices by JAX's collectives and lax.ppermute only.
A program may use at most 320 MiB of HBM per device.

v0:
```python
import jax
import jax.numpy as jnp
from jax import lax
from jax.sharding import PartitionSpec as P

HEADS = 16
floor_score = -1e30
epsilon = 1e-05


def rms_scaled(row_data, gain):
    values = row_data.astype(jnp.float32)
    return values * lax.rsqrt(jnp.mean(values * values, axis=-1, keepdims=True) + epsilon) * gain


def body(
    tokens, attn_gain, w_qkv, w_out, mlp_gain, w_gate_up, w_down, kv_cache, block_owner, block_fill
):
    groups = lax.axis_size("grp")
    row_count, feature_count = tokens.shape
    head_count = HEADS
    head_dim = feature_count // head_count
    per_group = row_count // groups
    score_scale = head_dim ** (-0.5)
    normed = rms_scaled(tokens, attn_gain).astype(jnp.bfloat16)
    qkv = jnp.dot(normed, w_qkv, preferred_element_type=jnp.float32).astype(jnp.bfloat16)
    sent_qkv, sent_input = (
        lax.all_to_all(
            qkv.reshape(per_group, groups, 3 * feature_count),
            "grp",
            split_axis=1,
            concat_axis=1,
            tiled=True,
        ),
        lax.all_to_all(
            tokens.reshape(per_group, groups, feature_count),
            "grp",
            split_axis=1,
            concat_axis=1,
            tiled=True,
        ),
    )
    served_qkv = sent_qkv.reshape(row_count, 3 * feature_count)
    served_input = sent_input.reshape(row_count, feature_count)
    query_own = served_qkv[:, :feature_count]
    key_own = served_qkv[:, feature_count : 2 * feature_count]
    value_own = served_qkv[:, 2 * feature_count :]
    offset = lax.axis_index("seq") * row_count
    query_all = lax.all_gather(query_own, "seq", axis=0, tiled=True)
    group_rows = query_all.shape[0]
    blocks, _, span, _ = kv_cache.shape
    key_block = kv_cache[:, 0].reshape(blocks, span, head_count, head_dim)
    value_block = kv_cache[:, 1].reshape(blocks, span, head_count, head_dim)
    query_blocks = query_all[block_owner].reshape(blocks, head_count, head_dim)
    scores = (
        jnp.einsum("bhd,bthd->bht", query_blocks, key_block, preferred_element_type=jnp.float32)
        * score_scale
    )
    is_valid = (
        lax.broadcasted_iota(jnp.int32, (blocks, head_count, span), 2) < block_fill[:, None, None]
    )
    masked = jnp.where(is_valid, scores, floor_score)
    block_max = jnp.max(masked, axis=2)
    weights = jnp.where(is_valid, jnp.exp(masked - block_max[:, :, None]), 0.0).astype(jnp.bfloat16)
    block_total = jnp.sum(weights.astype(jnp.float32), axis=2)
    block_sum = jnp.einsum(
        "bht,bthd->bhd", weights, value_block, preferred_element_type=jnp.float32
    )
    member = block_owner[None, :] == lax.broadcasted_iota(jnp.int32, (group_rows, blocks), 0)
    local_max = jnp.max(jnp.where(member[:, :, None], block_max[None, :, :], floor_score), axis=1)
    factor = jnp.exp(block_max - local_max[block_owner])
    member_table = member.astype(jnp.float32)
    local_total = jnp.dot(member_table, block_total * factor, precision=lax.Precision.HIGHEST)
    local_sum = jnp.dot(
        member_table,
        (block_sum * factor[:, :, None]).reshape(blocks, feature_count),
        precision=lax.Precision.HIGHEST,
    )
    own_max = lax.dynamic_slice_in_dim(local_max, offset, row_count, 0)
    own_total = lax.dynamic_slice_in_dim(local_total, offset, row_count, 0)
    own_sum = lax.dynamic_slice_in_dim(local_sum, offset, row_count, 0)
    query_float = query_own.astype(jnp.float32).reshape(row_count, head_count, head_dim)
    key_float = key_own.astype(jnp.float32).reshape(row_count, head_count, head_dim)
    own_score = jnp.sum(query_float * key_float, axis=2) * score_scale
    joined = jnp.maximum(own_max, own_score)
    keep_weight = jnp.exp(own_max - joined)
    own_weight = jnp.exp(own_score - joined)
    new_total = own_total * keep_weight + own_weight
    new_sum = own_sum.reshape(row_count, head_count, head_dim) * keep_weight[:, :, None]
    new_sum = (
        new_sum
        + value_own.astype(jnp.float32).reshape(row_count, head_count, head_dim)
        * own_weight[:, :, None]
    )
    local_max = lax.dynamic_update_slice_in_dim(local_max, joined, offset, 0)
    local_total = lax.dynamic_update_slice_in_dim(local_total, new_total, offset, 0)
    local_sum = lax.dynamic_update_slice_in_dim(
        local_sum, new_sum.reshape(row_count, feature_count), offset, 0
    )
    local_max, local_total, local_sum = (local_max, local_total, local_sum)
    maxima = lax.pmax(local_max, "seq")
    factor = jnp.exp(local_max - maxima)
    scaled_sum = (
        local_sum.reshape(local_sum.shape[0], head_count, head_dim) * factor[:, :, None]
    ).reshape(local_sum.shape)
    totals, weighted = (
        lax.psum_scatter(local_total * factor, "seq", scatter_dimension=0, tiled=True),
        lax.psum_scatter(scaled_sum, "seq", scatter_dimension=0, tiled=True),
    )
    scaled = weighted.reshape(weighted.shape[0], head_count, head_dim) / totals[:, :, None]
    context = scaled.reshape(weighted.shape[0], feature_count).astype(jnp.bfloat16)
    mixed_rows = served_input.astype(jnp.float32) + jnp.dot(
        context, w_out, preferred_element_type=jnp.float32
    )
    normed_mlp = rms_scaled(mixed_rows, mlp_gain).astype(jnp.bfloat16)
    rows_piece = lax.all_gather(normed_mlp, "seq", axis=0, tiled=True)
    gate_part = jnp.dot(rows_piece, w_gate_up[0], preferred_element_type=jnp.float32)
    up_part = jnp.dot(rows_piece, w_gate_up[1], preferred_element_type=jnp.float32)
    hidden = (jax.nn.silu(gate_part) * up_part).astype(jnp.bfloat16)
    partial_value = jnp.dot(hidden, w_down, preferred_element_type=jnp.float32)
    residual, partial_value = (mixed_rows, partial_value)
    down_sum = lax.psum_scatter(partial_value, "seq", scatter_dimension=0, tiled=True)
    output = (residual + down_sum).astype(jnp.bfloat16)
    returned = lax.all_to_all(
        output.reshape(per_group, groups, feature_count),
        "grp",
        split_axis=1,
        concat_axis=1,
        tiled=True,
    )
    return returned.reshape(row_count, feature_count)


def solution(mesh):
    in_specs = (
        P(("grp", "seq"), None),
        P(),
        P(),
        P(),
        P(),
        P(None, None, "seq"),
        P("seq", None),
        P(("grp", "seq"), None, None, None),
        P(("grp", "seq")),
        P(("grp", "seq")),
    )
    out_specs = P(("grp", "seq"), None)
    return jax.shard_map(body, mesh=mesh, in_specs=in_specs, out_specs=out_specs, check_vma=False)
```

profile of v0, /device:TPU:2, one launch (start us, length us, event | category | flops | bytes accessed | tf_op | source)
XLA Modules:
  0.0 860.8 jit_solution(14917239014895460157)
XLA Ops:
  6.5 1.0 fusion.20
  7.5 3.8 fusion
  11.4 0.5 broadcast.73
  11.8 0.7 reduce
  12.5 0.6 reshape.124
  13.1 4.5 all-to-all-start.1
  17.6 0.1 iota_compare_fusion.1
  17.7 4.0 fusion.39
  21.7 4.1 copy.67
  25.8 5.3 reshape_squeeze.7
  31.1 52.9 %all-gather = bf16[64,4,1024]{2,1,0:T(4,128)(2,1)S(1)} all-gather(bf16[1,4,1024]{2,1,0:T(4,128)(2,1)S(1)} %slice_bitcast_fusion), channel_id=1, replica_groups=mesh['grp'=4,'seq'=64] {'seq'}, dimensions={0}, use_global_device_ids=true | all-gather | bytes 532480 | tf_op jit(solution)/shard_map/all_gather | solution.py:49
  84.0 0.1 reshape.110
  84.1 0.6 gather_fusion
  84.7 0.1 reshape.118
  84.8 2.8 fusion.40
  87.6 0.2 fusion.13
  87.8 0.2 convert_reduce_fusion
  88.0 0.1 select_reduce_fusion
  88.1 0.1 copy.53
  88.2 0.6 gather_fusion.1
  88.8 0.2 fusion.25
  89.0 0.1 constant_dynamic-slice_fusion.1
  89.1 0.1 copy.72
  89.2 0.1 mul.127
  89.3 0.1 reduce_sum.37
  89.4 0.1 mul.130
  89.4 0.1 mul.131
  89.5 0.1 mul.133
  89.6 0.1 mul.134
  89.7 2.8 fusion.1
  92.5 0.1 broadcast_multiply_fusion
  92.6 0.1 reshape.87
  92.7 0.7 fusion.26
  93.4 0.1 copy.58
  93.5 0.3 dynamic_update_slice.11
  93.8 0.1 copy.55
  93.8 0.3 dynamic_update_slice.10
  94.1 244.1 %pmax.7 = f32[256,16]{0,1:T(8,128)S(1)} all-reduce(f32[256,16]{0,1:T(8,128)S(1)} %dynamic_update_slice.10), channel_id=1, replica_groups=mesh['grp'=4,'seq'=64] {'seq'}, use_global_device_ids=true, to_apply=%region_4.5 | all-reduce | flops 4096 | bytes 32768 | tf_op jit(solution)/shard_map/pmax | solution.py:101
  338.2 0.6 fusion.38
  338.8 1.1 mul.136
  339.8 2.6 copy.56
  342.5 2.4 mul.138
  344.9 0.0 all-reduce.6.cloned.1.call-update
  344.9 0.6 reduce.1
  345.6 0.6 reshape.126
  346.2 4.8 all-to-all-start
  351.0 0.6 dynamic-slice
  352.2 4.1 all-to-all-done
  356.3 246.3 %all-reduce.1 = f32[256,16]{0,1:T(8,128)S(1)} all-reduce(f32[256,16]{0,1:T(8,128)} %get-tuple-element.5), channel_id=3, replica_groups=mesh['grp'=4,'seq'=64] {'seq'}, use_global_device_ids=true, to_apply=%region_7.8.clone | all-reduce | flops 4096 | bytes 32768
  602.6 0.1 constant_dynamic-slice_fusion
  602.7 0.1 copy.59
  602.7 0.1 div.22
  602.8 0.1 div.23
  602.9 1.3 multiply_reduce_fusion
  604.2 0.1 fusion.28
  604.3 52.7 %all-gather.1 = bf16[64,4,1024]{2,1,0:T(4,128)(2,1)S(1)} all-gather(bf16[1,4,1024]{2,1,0:T(4,128)(2,1)S(1)} %fusion.28), channel_id=1, replica_groups=mesh['grp'=4,'seq'=64] {'seq'}, dimensions={0}, use_global_device_ids=true | all-gather | bytes 532480 | tf_op jit(solution)/shard_map/all_gather | solution.py:116
  657.0 0.1 reshape.112
  657.1 0.3 fusion.7
  657.4 1.9 fusion.4
  659.3 183.2 %all-reduce.8.cloned.1.call-done = f32[256,1024]{1,0:T(8,128)} async-done(((f32[256,1024]{1,0:T(8,128)}), f32[256,1024]{1,0:T(8,128)}) %all-reduce.8.cloned.1.call-update) | async-done | bytes 1048592
  842.5 0.8 fusion.29
  843.3 0.6 reduce.2
  843.9 9.4 %all_to_all.15 = bf16[4,2,512]{2,1,0:T(2,128)(2,1)S(1)} all-to-all(bf16[4,2,512]{2,1,0:T(2,128)(2,1)S(1)} %reshape.128), channel_id=1, replica_groups=mesh['grp'=4,'seq'=64] {'grp'}, dimensions={0} | all-to-all | bytes 16384 | tf_op jit(solution)/shard_map/all_to_all | solution.py:124
  853.3 0.6 copy.84
  (38 shorter events, 0.3 us)
Async XLA Ops:
  6.5 596.4 %copy-start = (bf16[1024,1024]{1,0:T(8,128)(2,1)S(1)}, bf16[1024,1024]{1,0:T(8,128)(2,1)}, u32[]{:S(2)}) copy-start(bf16[1024,1024]{1,0:T(8,128)(2,1)} %param.13) | copy-start | bytes 6291460
  7.5 10.1 %copy-start.6 = (s32[12]{0:T(128)S(1)}, s32[12]{0:T(128)}, u32[]{:S(2)}) copy-start(s32[12]{0:T(128)} %param.18) | copy-start | bytes 148
  13.1 17.9 %all-to-all-start.1 = ((bf16[4,2,1536]{2,1,0:T(2,128)(2,1)}), bf16[4,2,1536]{2,1,0:T(2,128)(2,1)S(1)}, u32[]{:S(2)}, u32[]{:S(2)}) async-start(bf16[4,2,1536]{2,1,0:T(2,128)(2,1)} %reshape.124), calls=%async_computation.1 | async-start | bytes 49152 | tf_op jit(solution)/shard_map/all_to_all | solution.py:28
  17.6 585.3 %all-reduce.6.cloned.1.call-start = ((), (), s32[]{:S(2)}) async-start(), calls=%async_computation.3 | async-start | bytes 2097152
  31.1 56.6 %copy-start.5 = (s32[12]{0:T(128)S(1)}, s32[12]{0:T(128)}, u32[]{:S(2)}) copy-start(s32[12]{0:T(128)} %param.19) | copy-start | bytes 148
  339.8 5.1 copy-start.3
  339.8 11.2 %copy-start.7 = (u32[256]{0:T(256)S(1)}, u32[256]{0:T(256)}, u32[]{:S(2)}) copy-start(u32[256]{0:T(256)} %constant.36) | copy-start | bytes 3076
  344.9 259.3 %copy-start.4 = (f32[1024]{0:T(1024)S(1)}, f32[1024]{0:T(1024)}, u32[]{:S(2)}) copy-start(f32[1024]{0:T(1024)} %param.14) | copy-start | bytes 12292
  344.9 312.2 %copy-start.1 = (bf16[2,1024,64]{1,2,0:T(8,128)(2,1)S(1)}, bf16[2,1024,64]{1,2,0:T(8,128)(2,1)}, u32[]{:S(2)}) copy-start(bf16[2,1024,64]{1,2,0:T(8,128)(2,1)} %param.15) | copy-start | bytes 786436
  344.9 312.5 %copy-start.2 = (bf16[64,1024]{1,0:T(8,128)(2,1)S(1)}, bf16[64,1024]{1,0:T(8,128)(2,1)}, u32[]{:S(2)}) copy-start(bf16[64,1024]{1,0:T(8,128)(2,1)} %param.16) | copy-start | bytes 393220
  346.2 10.1 %all-to-all-start = ((bf16[4,2,512]{2,1,0:T(2,128)(2,1)}), bf16[4,2,512]{2,1,0:T(2,128)(2,1)S(1)}, u32[]{:S(2)}, u32[]{:S(2)}) async-start(bf16[4,2,512]{2,1,0:T(2,128)(2,1)} %reshape.126), calls=%async_computation | async-start | bytes 16384 | tf_op jit(solution)/shard_map/all_to_all | solution.py:35
  351.0 491.5 %all-reduce.8.cloned.1.call-start = ((), (), s32[]{:S(2)}) async-start(), calls=%async_computation.4 | async-start | bytes 2097152
Sparse Core Ops, SparseCore 0:
  345.0 188.2 all-reduce.5
  659.4 183.0 all-reduce.7
where the time goes:
time: 862 us; the launch traced here: 861 us
  blocking collectives  605 us (70%)
  waiting for transfers between devices  187 us (22%)
  local copies, waits for them, and re-layouts  23.4 us (3%)
  between operations  14.3 us (2%)
  matrix products  13.7 us (2%)
  starting transfers between devices  9.26 us (1%)
    unnamed x1, blocking collectives  246 us
    pmax x1, blocking collectives, body(): maxima = lax.pmax(local_max, 'seq')  244 us
    unnamed x4, waiting for transfers between devices  183 us
    all_gather x1, blocking collectives, body(): query_all = lax.all_gather(query_own, 'seq', axis=0, tiled=True)  52.9 us
    all_gather x1, blocking collectives, body(): rows_piece = lax.all_gather(normed_mlp, 'seq', axis=0, tiled=True)  52.7 us
  transfers between devices with their start and end apart: 4, of which 2 were waited for; matrix products, arithmetic and copies ran while one was open for 2% of the time, Pallas kernels for 0%

commit v1 on v0

--- a/solution.py
+++ b/solution.py
@@ -6,6 +6,13 @@
 HEADS = 16
 floor_score = -1e30
 epsilon = 1e-05
+
+
+def all_by_exchange(x, name, dim):
+    size = lax.axis_size(name)
+    blocks = jnp.stack([x for _ in range(size)])
+    blocks = lax.all_to_all(blocks, name, split_axis=0, concat_axis=0)
+    return jnp.concatenate(blocks, axis=dim)
 
 
 def rms_scaled(row_data, gain):
@@ -113,7 +120,7 @@
         context, w_out, preferred_element_type=jnp.float32
     )
     normed_mlp = rms_scaled(mixed_rows, mlp_gain).astype(jnp.bfloat16)
-    rows_piece = lax.all_gather(normed_mlp, "seq", axis=0, tiled=True)
+    rows_piece = all_by_exchange(normed_mlp, "seq", 0)
     gate_part = jnp.dot(rows_piece, w_gate_up[0], preferred_element_type=jnp.float32)
     up_part = jnp.dot(rows_piece, w_gate_up[1], preferred_element_type=jnp.float32)
     hidden = (jax.nn.silu(gate_part) * up_part).astype(jnp.bfloat16)

time: 862 us -> 835 us (0.969)
  blocking collectives: 605 us -> 582 us
    all_gather x1 -> x0, blocking collectives: 52.7 us -> none  [body(): rows_piece = lax.all_gather(normed_mlp, 'seq', axis=0, tiled=True)]
    all_to_all x0 -> x1, blocking collectives: none -> 29.1 us  [all_by_exchange(): blocks = lax.all_to_all(blocks, name, split_axis=0, concat_axis=0)]
where the time goes in v1:
time: 835 us; the launch traced here: 834 us
  blocking collectives  582 us (70%)
  waiting for transfers between devices  184 us (22%)
  local copies, waits for them, and re-layouts  23.5 us (3%)
  between operations  14.3 us (2%)
  matrix products  13.7 us (2%)
  starting transfers between devices  9.26 us (1%)
    unnamed x1, blocking collectives  246 us
    pmax x1, blocking collectives, body(): maxima = lax.pmax(local_max, 'seq')  244 us
    unnamed x4, waiting for transfers between devices  180 us
    all_gather x1, blocking collectives, body(): query_all = lax.all_gather(query_own, 'seq', axis=0, tiled=True)  52.9 us
    all_to_all x1, blocking collectives, all_by_exchange(): blocks = lax.all_to_all(blocks, name, split_axis=0, concat_axis=0)  29.1 us
  transfers between devices with their start and end apart: 4, of which 2 were waited for; matrix products, arithmetic and copies ran while one was open for 2% of the time, Pallas kernels for 0%

profile of v1, /device:TPU:2, one launch (start us, length us, event | category | flops | bytes accessed | tf_op | source)
XLA Modules:
  0.0 834.3 jit_solution(6617653073184084321)
XLA Ops:
  6.5 1.0 fusion.20
  7.5 3.8 fusion
  11.4 0.5 broadcast.75
  11.8 0.7 reduce
  12.5 0.6 reshape.128
  13.1 4.5 all-to-all-start.1
  17.6 0.1 iota_compare_fusion.1
  17.7 4.0 fusion.38
  21.7 4.1 copy.67
  25.8 5.3 reshape_squeeze.7
  31.1 52.9 %all-gather = bf16[64,4,1024]{2,1,0:T(4,128)(2,1)S(1)} all-gather(bf16[1,4,1024]{2,1,0:T(4,128)(2,1)S(1)} %slice_bitcast_fusion), channel_id=1, replica_groups=mesh['grp'=4,'seq'=64] {'seq'}, dimensions={0}, use_global_device_ids=true | all-gather | bytes 532480 | tf_op jit(solution)/shard_map/all_gather | solution.py:56
  84.0 0.1 reshape.116
  84.1 0.6 gather_fusion
  84.7 0.1 reshape.122
  84.8 2.8 fusion.39
  87.6 0.2 fusion.13
  87.8 0.2 convert_reduce_fusion
  88.0 0.1 select_reduce_fusion
  88.1 0.1 copy.53
  88.2 0.6 gather_fusion.1
  88.8 0.2 fusion.25
  89.0 0.1 constant_dynamic-slice_fusion.1
  89.1 0.1 copy.72
  89.2 0.1 mul.127
  89.3 0.1 reduce_sum.37
  89.4 0.1 mul.130
  89.4 0.1 mul.131
  89.5 0.1 mul.133
  89.6 0.1 mul.134
  89.7 2.8 fusion.1
  92.5 0.1 broadcast_multiply_fusion
  92.6 0.1 reshape.92
  92.7 0.7 fusion.26
  93.4 0.1 copy.58
  93.5 0.3 dynamic_update_slice.11
  93.8 0.1 copy.55
  93.8 0.3 dynamic_update_slice.10
  94.1 244.1 %pmax.7 = f32[256,16]{0,1:T(8,128)S(1)} all-reduce(f32[256,16]{0,1:T(8,128)S(1)} %dynamic_update_slice.10), channel_id=1, replica_groups=mesh['grp'=4,'seq'=64] {'seq'}, use_global_device_ids=true, to_apply=%region_4.5 | all-reduce | flops 4096 | bytes 32768 | tf_op jit(solution)/shard_map/pmax | solution.py:108
  338.2 0.6 fusion.37
  338.8 1.1 mul.136
  339.8 2.6 copy.56
  342.5 2.4 mul.138
  345.0 0.7 reduce.1
  345.6 0.6 reshape.130
  346.2 4.8 all-to-all-start
  351.0 0.6 dynamic-slice
  352.3 4.1 all-to-all-done
  356.4 246.2 %all-reduce.1 = f32[256,16]{0,1:T(8,128)S(1)} all-reduce(f32[256,16]{0,1:T(8,128)} %get-tuple-element.5), channel_id=3, replica_groups=mesh['grp'=4,'seq'=64] {'seq'}, use_global_device_ids=true, to_apply=%region_7.8.clone | all-reduce | flops 4096 | bytes 32768
  602.6 0.1 constant_dynamic-slice_fusion
  602.7 0.1 copy.59
  602.7 0.1 div.22
  602.8 0.1 div.23
  602.9 1.3 multiply_reduce_fusion
  604.2 0.1 multiply_convert_fusion
  604.3 0.1 stack.2
  604.4 29.1 %all_to_all.20 = bf16[64,4,1024]{2,1,0:T(4,128)(2,1)S(1)} all-to-all(bf16[64,4,1024]{2,1,0:T(4,128)(2,1)S(1)} %stack.2), channel_id=1, replica_groups=mesh['grp'=4,'seq'=64] {'seq'}, dimensions={0} | all-to-all | bytes 1048576 | tf_op jit(solution)/shard_map/all_to_all | solution.py:14
  633.5 0.1 reshape.93
  633.7 0.3 fusion.7
  634.0 1.9 fusion.4
  635.9 180.1 %all-reduce.8.cloned.1.call-done = f32[256,1024]{1,0:T(8,128)} async-done(((f32[256,1024]{1,0:T(8,128)}), f32[256,1024]{1,0:T(8,128)}) %all-reduce.8.cloned.1.call-update) | async-done | bytes 1048592
  816.0 0.8 fusion.28
  816.8 0.6 reduce.2
  817.4 9.4 %all_to_all.21 = bf16[4,2,512]{2,1,0:T(2,128)(2,1)S(1)} all-to-all(bf16[4,2,512]{2,1,0:T(2,128)(2,1)S(1)} %reshape.132), channel_id=1, replica_groups=mesh['grp'=4,'seq'=64] {'grp'}, dimensions={0} | all-to-all | bytes 16384 | tf_op jit(solution)/shard_map/all_to_all | solution.py:131
  826.8 0.6 copy.84
  (39 shorter events, 0.3 us)
Async XLA Ops:
  6.5 596.4 %copy-start = (bf16[1024,1024]{1,0:T(8,128)(2,1)S(1)}, bf16[1024,1024]{1,0:T(8,128)(2,1)}, u32[]{:S(2)}) copy-start(bf16[1024,1024]{1,0:T(8,128)(2,1)} %param.13) | copy-start | bytes 6291460
  7.5 10.1 %copy-start.6 = (s32[12]{0:T(128)S(1)}, s32[12]{0:T(128)}, u32[]{:S(2)}) copy-start(s32[12]{0:T(128)} %param.18) | copy-start | bytes 148
  13.1 17.9 %all-to-all-start.1 = ((bf16[4,2,1536]{2,1,0:T(2,128)(2,1)}), bf16[4,2,1536]{2,1,0:T(2,128)(2,1)S(1)}, u32[]{:S(2)}, u32[]{:S(2)}) async-start(bf16[4,2,1536]{2,1,0:T(2,128)(2,1)} %reshape.128), calls=%async_computation.1 | async-start | bytes 49152 | tf_op jit(solution)/shard_map/all_to_all | solution.py:35
  17.6 585.3 %all-reduce.6.cloned.1.call-start = ((), (), s32[]{:S(2)}) async-start(), calls=%async_computation.4 | async-start | bytes 2097152
  31.1 56.6 %copy-start.5 = (s32[12]{0:T(128)S(1)}, s32[12]{0:T(128)}, u32[]{:S(2)}) copy-start(s32[12]{0:T(128)} %param.19) | copy-start | bytes 148
  339.8 5.1 copy-start.3
  339.8 11.2 %copy-start.7 = (u32[256]{0:T(256)S(1)}, u32[256]{0:T(256)}, u32[]{:S(2)}) copy-start(u32[256]{0:T(256)} %constant.36) | copy-start | bytes 3076
  344.9 259.3 %copy-start.4 = (f32[1024]{0:T(1024)S(1)}, f32[1024]{0:T(1024)}, u32[]{:S(2)}) copy-start(f32[1024]{0:T(1024)} %param.14) | copy-start | bytes 12292
  344.9 288.8 %copy-start.1 = (bf16[2,1024,64]{1,2,0:T(8,128)(2,1)S(1)}, bf16[2,1024,64]{1,2,0:T(8,128)(2,1)}, u32[]{:S(2)}) copy-start(bf16[2,1024,64]{1,2,0:T(8,128)(2,1)} %param.15) | copy-start | bytes 786436
  344.9 289.1 %copy-start.2 = (bf16[64,1024]{1,0:T(8,128)(2,1)S(1)}, bf16[64,1024]{1,0:T(8,128)(2,1)}, u32[]{:S(2)}) copy-start(bf16[64,1024]{1,0:T(8,128)(2,1)} %param.16) | copy-start | bytes 393220
  346.2 10.1 %all-to-all-start = ((bf16[4,2,512]{2,1,0:T(2,128)(2,1)}), bf16[4,2,512]{2,1,0:T(2,128)(2,1)S(1)}, u32[]{:S(2)}, u32[]{:S(2)}) async-start(bf16[4,2,512]{2,1,0:T(2,128)(2,1)} %reshape.130), calls=%async_computation | async-start | bytes 16384 | tf_op jit(solution)/shard_map/all_to_all | solution.py:42
  351.0 465.0 %all-reduce.8.cloned.1.call-start = ((), (), s32[]{:S(2)}) async-start(), calls=%async_computation.5 | async-start | bytes 2097152
Sparse Core Ops, SparseCore 0:
  345.0 188.5 all-reduce.5
  636.0 179.9 all-reduce.7
